TPU v7x, 128 devices: a whole 4x4x4 slice. The times are simulated.
128 devices in a mesh: dom: 16 (over x, y), blk: 8 (over z, core).
Axes of the slice: x: 4, y: 4, z: 4, core: 2. Of those that a mesh axis runs over, the one named last changes fastest.
Arguments:
- node_features: bfloat16 [32768, 512], P(('dom', 'blk')), may hold values from -6 to 6
- norm_gain: float32 [512], replicated, may hold values from 0.25 to 1.75
- w_query: bfloat16 [512, 512], replicated, may hold values from -0.25 to 0.25
- w_key: bfloat16 [512, 512], replicated, may hold values from -0.25 to 0.25
- w_value: bfloat16 [512, 512], replicated, may hold values from -0.25 to 0.25
- w_out: bfloat16 [512, 512], replicated, may hold values from -1.5 to 1.5
- w_message: bfloat16 [512, 512], replicated, may hold values from -1 to 1
- node_cluster: int32 [32768], P(('dom', 'blk')), may hold values from 0 to 15
- block_pattern: int32 [128, 8], P(('dom', 'blk')), may hold values from 0 to 1, as said below
- send_rows: int32 [2048, 128], P(('dom', 'blk')), may hold values from 0 to 255
- send_counts: int32 [2048], P(('dom', 'blk')), may hold values from 32 to 128, as said below
- edge_src: int32 [524288], P(('dom', 'blk')), may hold values from 0 to 2047
- edge_dst: int32 [524288], P(('dom', 'blk')), may hold values from 0 to 255
- out_grad: bfloat16 [32768, 512], P(('dom', 'blk')), may hold values from -6 to 6
Outputs:
- layer_out: bfloat16 [32768, 512], P(('dom', 'blk'))
- feature_grad: bfloat16 [32768, 512], P(('dom', 'blk'))
- weight_grads: float32 [5, 512, 512], replicated
- gain_grad: float32 [512], replicated
Inputs may be any that keep to these rules, and one draw needn't show every extreme that they name: `block_pattern`: row g has a 1 at column (g mod 8); other entries are 0 or 1. `send_counts`: entry g * 16 + p is how many leading slots of device g's block to dom peer p are live; every device has one peer whose block has all 128 slots live.
All inputs are finite; a program needn't handle non-finite values.
Results may differ from a plain program's by a relative error of at most 0.013.
Values may be sent and summed in bfloat16 or wider, within the bound.
No kernel may reach another device: no remote copies, remote signals or barrier semaphores. Data moves between devices by JAX's collectives and lax.ppermute only.
A program may use at most 128 MiB of HBM per device.

v0:
```python
from functools import partial
import jax
import jax.numpy as jnp
from jax import lax
from jax.sharding import PartitionSpec as P

HEADS = 8
HEAD_DIM = 64
epsilon = 1e-06
score_shift = 8.0


def settle(array):
    return lax.optimization_barrier(array.astype(jnp.bfloat16)).astype(jnp.float32)


def rms_norm(features, norm_gain):
    scaling = lax.rsqrt(jnp.mean(features * features, axis=-1, keepdims=True) + epsilon)
    return features * scaling * norm_gain


def head_norm(projected):
    head_view = projected.reshape(projected.shape[0], HEADS, HEAD_DIM)
    scaling = lax.rsqrt(jnp.mean(head_view * head_view, axis=-1, keepdims=True) + epsilon)
    return (head_view * scaling).reshape(projected.shape)


def block_weights(query_heads, key_heads, allowed):
    scaling = score_shift / HEAD_DIM
    scores = (
        jnp.einsum("rhe,khe->hrk", query_heads, key_heads, preferred_element_type=jnp.float32)
        * scaling
    )
    return jnp.where(allowed[None], jnp.exp(scores - score_shift), 0.0)


def attend_piece(running, shard_piece, offset, query_heads, query_labels, pattern_row, skip_empty):
    key_rows, value_rows, key_labels = shard_piece
    row_count = query_heads.shape[0]
    piece_rows = key_rows.shape[0]
    part_count = max(piece_rows // row_count, 1)
    block_index = jnp.arange(pattern_row.shape[0], dtype=jnp.int32)
    for position in range(part_count):
        first_row = position * piece_rows // part_count
        last_row = (position + 1) * piece_rows // part_count
        part_rows = last_row - first_row
        key_part = key_rows[first_row:last_row].reshape(part_rows, HEADS, HEAD_DIM)
        value_part = value_rows[first_row:last_row].reshape(part_rows, HEADS, HEAD_DIM)
        label_part = key_labels[first_row:last_row]
        owners = (offset + first_row + jnp.arange(part_rows, dtype=jnp.int32)) // row_count
        block_flags = jnp.sum(
            jnp.where(owners[:, None] == block_index[None, :], pattern_row[None, :], 0), axis=1
        )
        allowed = (query_labels[:, None] == label_part[None, :]) & (block_flags[None, :] == 1)

        def accumulate(current, key_part=key_part, value_part=value_part, allowed=allowed):
            numer, denom = current
            weights = block_weights(query_heads, key_part, allowed)
            denom = denom + jnp.sum(weights, axis=2).T
            numer = numer + jnp.einsum(
                "hrk,khe->rhe",
                weights.astype(jnp.bfloat16),
                value_part,
                preferred_element_type=jnp.float32,
            )
            return (numer, denom)

        running = accumulate(running)
    return running


def pair_gradients(query_heads, grad_heads, correction, key_part, value_part, allowed):
    scaling = score_shift / HEAD_DIM
    weights = block_weights(query_heads, key_part, allowed)
    grad_dots = jnp.einsum(
        "rhe,khe->hrk", grad_heads, value_part, preferred_element_type=jnp.float32
    )
    slopes = (weights * (grad_dots - correction.T[:, :, None])).astype(jnp.bfloat16)
    dq_part = (
        jnp.einsum("hrk,khe->rhe", slopes, key_part, preferred_element_type=jnp.float32) * scaling
    )
    dk_part = (
        jnp.einsum("hrk,rhe->khe", slopes, query_heads, preferred_element_type=jnp.float32)
        * scaling
    )
    dv_part = jnp.einsum(
        "hrk,rhe->khe", weights.astype(jnp.bfloat16), grad_heads, preferred_element_type=jnp.float32
    )
    return (dq_part, dk_part, dv_part)


def key_block(
    query_heads, grad_heads, correction, query_labels, skip_empty, dq_total, block_inputs
):
    key_part, value_part, label_part, block_flag = block_inputs
    row_count = query_heads.shape[0]
    allowed = (query_labels[:, None] == label_part[None, :]) & (block_flag == 1)
    dq_part, dk_part, dv_part = pair_gradients(
        query_heads, grad_heads, correction, key_part, value_part, allowed
    )
    flat_terms = (dk_part.reshape(row_count, -1), dv_part.reshape(row_count, -1))
    return (dq_total + settle(dq_part), flat_terms)


def local(
    node_features,
    norm_gain,
    w_query,
    w_key,
    w_value,
    w_out,
    w_message,
    node_cluster,
    block_pattern,
    send_rows,
    send_counts,
    edge_src,
    edge_dst,
    out_grad,
):
    row_count = node_features.shape[0]
    feat_width = node_features.shape[1]
    peer_count = lax.axis_size("dom")
    block_count = lax.axis_size("blk")
    slot_count = send_rows.shape[1]
    features = node_features.astype(jnp.float32)
    normed_f, norm_pull = jax.vjp(rms_norm, features, norm_gain)
    normed = normed_f.astype(jnp.bfloat16)
    live_slots = jnp.arange(slot_count, dtype=jnp.int32)[None, :] < send_counts[:, None]
    outgoing = jnp.where(live_slots[:, :, None], normed[send_rows], jnp.zeros((), jnp.bfloat16))
    incoming = lax.all_to_all(outgoing, "dom", split_axis=0, concat_axis=0, tiled=True)
    query_f, query_pull = jax.vjp(
        head_norm, jnp.dot(normed, w_query, preferred_element_type=jnp.float32)
    )
    key_f, key_pull = jax.vjp(head_norm, jnp.dot(normed, w_key, preferred_element_type=jnp.float32))
    queries = query_f.astype(jnp.bfloat16)
    key_flat = key_f.astype(jnp.bfloat16)
    value_flat = jnp.dot(normed, w_value, preferred_element_type=jnp.float32).astype(jnp.bfloat16)
    query_heads = queries.reshape(row_count, HEADS, HEAD_DIM)
    pattern_row = block_pattern[0]
    start_state = (
        jnp.zeros((row_count, HEADS, HEAD_DIM), jnp.float32),
        jnp.zeros((row_count, HEADS), jnp.float32),
    )
    fold_step = partial(
        attend_piece,
        query_heads=query_heads,
        query_labels=node_cluster,
        pattern_row=pattern_row,
        skip_empty=False,
    )
    key_set = None
    key_set = (
        lax.all_gather(key_flat, "blk", axis=0, tiled=True),
        lax.all_gather(value_flat, "blk", axis=0, tiled=True),
        lax.all_gather(node_cluster, "blk", axis=0, tiled=True),
    )
    numer, denom = fold_step(start_state, key_set, 0)
    slot_table = incoming.reshape(peer_count * slot_count, feat_width)
    pair_index = edge_src * row_count + edge_dst
    edge_counts = jnp.zeros((peer_count * slot_count * row_count,), jnp.int32).at[pair_index].add(1)
    edge_counts = edge_counts.reshape(peer_count * slot_count, row_count).astype(jnp.bfloat16)
    degree = jnp.maximum(
        jax.ops.segment_sum(jnp.ones(edge_dst.shape, jnp.float32), edge_dst, row_count), 1.0
    )
    neighbour_sum = jnp.einsum(
        "sr,sd->rd", edge_counts, slot_table, preferred_element_type=jnp.float32
    )
    mean_rows = (neighbour_sum / degree[:, None]).astype(jnp.bfloat16)
    local_term = jnp.dot(mean_rows, w_message, preferred_element_type=jnp.float32)
    attn_heads = (numer / denom[..., None]).astype(jnp.bfloat16)
    attn_rows = attn_heads.reshape(row_count, feat_width)
    attn_proj = jnp.dot(attn_rows, w_out, preferred_element_type=jnp.float32)
    layer_out = (features + local_term + attn_proj).astype(jnp.bfloat16)
    grad_attn = jnp.einsum(
        "rd,ed->re", out_grad, w_out, preferred_element_type=jnp.float32
    ).reshape(row_count, HEADS, HEAD_DIM)
    grad_heads = (grad_attn / denom[..., None]).astype(jnp.bfloat16)
    correction = jnp.sum(grad_attn * attn_heads.astype(jnp.float32), axis=-1) / denom
    key_rows, value_rows, key_labels = key_set
    block_inputs = (
        key_rows.reshape(block_count, row_count, HEADS, HEAD_DIM),
        value_rows.reshape(block_count, row_count, HEADS, HEAD_DIM),
        key_labels.reshape(block_count, row_count),
        pattern_row,
    )
    block_step = partial(key_block, query_heads, grad_heads, correction, node_cluster, False)
    dq_heads, (key_terms, value_terms) = lax.scan(
        block_step, jnp.zeros((row_count, HEADS, HEAD_DIM), jnp.float32), block_inputs
    )
    key_grad, value_grad = (
        lax.psum_scatter(
            key_terms.reshape(block_count * row_count, feat_width).astype(jnp.bfloat16),
            "blk",
            scatter_dimension=0,
            tiled=True,
        ).astype(jnp.float32),
        lax.psum_scatter(
            value_terms.reshape(block_count * row_count, feat_width).astype(jnp.bfloat16),
            "blk",
            scatter_dimension=0,
            tiled=True,
        ).astype(jnp.float32),
    )
    dq_flat = dq_heads.reshape(row_count, feat_width)
    dquery = query_pull(dq_flat)[0].astype(jnp.bfloat16)
    dkey = key_pull(key_grad)[0].astype(jnp.bfloat16)
    dvalue = value_grad.astype(jnp.bfloat16)
    dmessage = (
        jnp.einsum("rd,ed->re", out_grad, w_message, preferred_element_type=jnp.float32)
        / degree[:, None]
    ).astype(jnp.bfloat16)
    slot_grads = jnp.dot(edge_counts, dmessage, preferred_element_type=jnp.float32).astype(
        jnp.bfloat16
    )
    returned = lax.all_to_all(
        slot_grads.reshape(peer_count, slot_count, feat_width),
        "dom",
        split_axis=0,
        concat_axis=0,
        tiled=True,
    )
    returned = jnp.where(live_slots[:, :, None], returned.astype(jnp.float32), 0.0)
    halo_grad = jax.ops.segment_sum(
        returned.reshape(peer_count * slot_count, feat_width), send_rows.reshape(-1), row_count
    )
    dnormed = jnp.einsum("rd,ed->re", dquery, w_query, preferred_element_type=jnp.float32)
    dnormed = dnormed + jnp.einsum("rd,ed->re", dkey, w_key, preferred_element_type=jnp.float32)
    dnormed = dnormed + jnp.einsum("rd,ed->re", dvalue, w_value, preferred_element_type=jnp.float32)
    dnormed = dnormed + halo_grad
    dfeatures, gain_term = norm_pull(dnormed)
    feature_grad = (out_grad.astype(jnp.float32) + dfeatures).astype(jnp.bfloat16)
    weight_terms = jnp.stack(
        [
            jnp.einsum("rd,re->de", normed, dquery, preferred_element_type=jnp.float32),
            jnp.einsum("rd,re->de", normed, dkey, preferred_element_type=jnp.float32),
            jnp.einsum("rd,re->de", normed, dvalue, preferred_element_type=jnp.float32),
            jnp.einsum("rd,re->de", attn_rows, out_grad, preferred_element_type=jnp.float32),
            jnp.einsum("rd,re->de", mean_rows, out_grad, preferred_element_type=jnp.float32),
        ]
    )
    weight_sums, gain_sum = lax.psum((weight_terms, gain_term), ("dom", "blk"))
    return (layer_out, feature_grad, weight_sums, gain_sum)


def solution(mesh):
    placed = (
        P(("dom", "blk"), None),
        P(),
        P(),
        P(),
        P(),
        P(),
        P(),
        P(("dom", "blk")),
        P(("dom", "blk"), None),
        P(("dom", "blk"), None),
        P(("dom", "blk")),
        P(("dom", "blk")),
        P(("dom", "blk")),
        P(("dom", "blk"), None),
    )
    return jax.shard_map(
        local,
        mesh=mesh,
        in_specs=placed,
        out_specs=(P(("dom", "blk"), None), P(("dom", "blk"), None), P(), P()),
        check_vma=False,
    )
```

profile of v0, /device:TPU:1, one launch (start us, length us, event | category | flops | bytes accessed | tf_op | source)
XLA Modules:
  0.0 467.6 jit_solution(4525256311109926087)
XLA Ops:
  9.5 1.3 fusion.57
  15.0 2.1 copy.152
  18.3 13.1 %all-gather = s32[8,1,256]{2,1,0:T(1,128)S(1)} all-gather(s32[1,1,256]{2,1,0:T(1,128)S(1)} %bitcast.258), channel_id=1, replica_groups=mesh['dom'=16,'blk'=8] {'blk'}, dimensions={0}, use_global_device_ids=true | all-gather | bytes 9216 | tf_op jit(solution)/shard_map/all_gather | solution.py:156
  31.7 1.5 compare_and_fusion.1
  33.6 7.9 %all-gather.6.cloned.1.call-done = bf16[2048,512]{1,0:T(8,128)(2,1)} async-done(((bf16[256,512]{1,0:T(8,128)(2,1)}), bf16[2048,512]{1,0:T(8,128)(2,1)}) %all-gather.6.cloned.1.call-update) | async-done | bytes 2097168 | tf_op jit(solution)/shard_map/all_gather | solution.py:154
  41.5 2.5 fusion.54
  43.9 1.8 copy.156
  45.7 23.3 %all-gather.4.cloned.1.call-done = bf16[2048,512]{1,0:T(8,128)(2,1)} async-done(((bf16[256,512]{1,0:T(8,128)(2,1)}), bf16[2048,512]{1,0:T(8,128)(2,1)}) %all-gather.4.cloned.1.call-update) | async-done | bytes 2097168 | tf_op jit(solution)/shard_map/all_gather | solution.py:155
  69.0 2.8 fusion.55
  71.9 1.8 copy.150
  83.3 1.8 copy.174
  85.1 1.8 copy.173
  86.9 1.8 copy.177
  88.7 1.8 copy.176
  90.5 1.8 fusion.64
  101.9 6.1 %reshape.794 = bf16[8,256,8,64]{3,2,1,0:T(8,128)(2,1)} reshape(bf16[2048,512]{1,0:T(8,128)(2,1)} %all-gather.6.cloned.1.call-done) | data formatting | bytes 4194304 | tf_op jit(solution)/shard_map/reshape | solution.py:182
  108.0 5.1 %copy.182 = bf16[8,256,8,64]{1,3,2,0:T(8,128)(2,1)} copy(bf16[8,256,8,64]{3,2,1,0:T(8,128)(2,1)} %reshape.794) | data formatting | bytes 4194304
  113.1 6.1 %reshape.795 = bf16[8,256,8,64]{3,2,1,0:T(8,128)(2,1)} reshape(bf16[2048,512]{1,0:T(8,128)(2,1)} %all-gather.4.cloned.1.call-done) | data formatting | bytes 4194304 | tf_op jit(solution)/shard_map/reshape | solution.py:183
  119.3 5.1 %copy.183 = bf16[8,256,8,64]{1,3,2,0:T(8,128)(2,1)} copy(bf16[8,256,8,64]{3,2,1,0:T(8,128)(2,1)} %reshape.795) | data formatting | bytes 4194304
  124.4 67.0 %while.17 = (s32[]{:T(128)}, f32[256,8,64]{0,2,1:T(8,128)S(1)}, bf16[8,256,512]{1,2,0:T(8,128)(2,1)}, bf16[8,256,512]{2,1,0:T(8,128)(2,1)}, bf16[8,256,8,64]{1,3...) while((s32[]{:T(128)}, f32[256,8,64]{0,2,1:T(8,128)S(1)}, ...), condition=%wide.region_23.24_spmd.clone, body=%wide.region_22.23_spmd.clone.sunk | while | flops 340262912 | bytes 15088305 | solution.py:188
  125.8 1.6 bitcast_select_fusion.2
  127.4 1.4 fusion.163
  134.1 1.6 bitcast_select_fusion.2
  135.7 1.4 fusion.163
  142.5 1.6 bitcast_select_fusion.2
  144.1 1.4 fusion.163
  148.0 1.2 fusion.164
  150.9 1.6 bitcast_select_fusion.2
  152.5 1.4 fusion.163
  159.2 1.6 bitcast_select_fusion.2
  160.8 1.4 fusion.163
  164.8 1.2 fusion.164
  167.6 1.6 bitcast_select_fusion.2
  169.2 1.4 fusion.163
  176.0 1.6 bitcast_select_fusion.2
  177.6 1.4 fusion.163
  184.4 1.6 bitcast_select_fusion.2
  186.0 1.4 fusion.163
  189.9 1.2 fusion.164
  191.4 4.0 copy.184
  196.1 7.5 %gather_fusion = bf16[2048,512]{1,0:T(8,128)(2,1)S(1)} fusion(bf16[256,512]{1,0:T(8,128)(2,1)S(1)} %fusion.38, s32[2048]{0:T(1024)S(1)} %fusion.48), kind=kCustom, calls=%fused_computation | custom fusion | bytes 4202496 | tf_op jit(solution)/shard_map/gather | solution.py:130
  203.7 1.5 broadcast_select_fusion
  205.2 6.6 %all-to-all-start = ((bf16[16,128,512]{2,1,0:T(8,128)(2,1)}), bf16[16,128,512]{2,1,0:T(8,128)(2,1)}, u32[]{:S(2)}, u32[]{:S(2)}) async-start(bf16[16,128,512]{2,1,0:T(8,128)(2,1)} %broadcast_select_fusion), calls=%async_computation | async-start | bytes 4194304 | tf_op jit(solution)/shard_map/all_to_all | solution.py:131
  212.6 22.4 %scatter_custom_fusion = s32[524288]{0:T(1024)S(1)} fusion(s32[4096]{0:T(1024)S(1)} %compare_select_fusion, s32[4096]{0:T(1024)S(1)} %broadcast.736, s32[]{:T(128)} %constant.148.clone.1), kind=kCustom, calls=%fused_computation.77 | custom fusion | flops 4096 | bytes 2097156 | tf_op jit(solution)/shard_map/scatter-add | solution.py:161
  236.1 1.5 convert_element_type.131
  237.6 28.8 %scatter_custom_fusion.1 = f32[256]{0:T(256)S(1)} fusion(s32[4096]{0:T(1024)S(1)} %copy-done.48, f32[4096]{0:T(1024)S(1)} %broadcast.737, f32[]{:T(128)} %constant.152.clone.1), kind=kCustom, calls=%fused_computation.188 | custom fusion | flops 4096 | bytes 1028 | tf_op jit(solution)/shard_map/scatter-add | solution.py:164
  266.4 2.4 convolution_convert_fusion
  268.8 6.6 %all-to-all-start.1 = ((bf16[16,128,512]{2,1,0:T(8,128)(2,1)}), bf16[16,128,512]{2,1,0:T(8,128)(2,1)S(1)}, u32[]{:S(2)}, u32[]{:S(2)}) async-start(bf16[16,128,512]{2,1,0:T(8,128)(2,1)} %bitcast.233), calls=%async_computation.3 | async-start | bytes 4194304 | tf_op jit(solution)/shard_map/all_to_all | solution.py:216
  275.4 3.4 fusion.21
  279.7 1.3 fusion.18
  281.1 2.0 convert_multiply_fusion.4
  283.1 2.1 copy.186
  287.1 2.0 copy.187
  289.2 1.5 fusion.41
  291.4 1.3 fusion.17
  292.7 2.3 fusion.16
  295.0 1.3 fusion.15
  296.2 1.3 fusion.14
  299.7 2.5 all-to-all-done.1
  302.2 2.5 convert_select_fusion
  306.9 13.5 %scatter_fusion = f32[256,512]{1,0:T(8,128)S(1)} fusion(f32[256,512]{1,0:T(8,128)S(1)} %convolution_add_fusion.7, s32[2048]{0:T(1024)S(1)} %bitcast.259, f32[2048,512]{1,0:T(8,128)} %bitcast.218), kind=kCustom, calls=%fused_computation.3 | custom fusion | flops 1048576 | bytes 12591104 | tf_op jit(solution)/shard_map/scatter-add | solution.py:224
  320.6 65.8 %psum.15 = f32[512]{0:T(512)} all-reduce(f32[512]{0:T(512)S(1)} %get-tuple-element.245), channel_id=1, replica_groups=mesh['dom'=16,'blk'=8] {'dom','blk'}, use_global_device_ids=true, to_apply=%region_32.33 | all-reduce | flops 512 | bytes 4096 | tf_op jit(solution)/shard_map/psum | solution.py:242
  387.3 67.9 %all-reduce.2.cloned.1.call-done = f32[5,512,512]{2,1,0:T(8,128)} async-done(((f32[5,512,512]{2,1,0:T(8,128)}), f32[5,512,512]{2,1,0:T(8,128)}) %all-reduce.2.cloned.1.call-update) | async-done | bytes 5242896 | tf_op jit(solution)/shard_map/psum | solution.py:242
  455.3 5.8 %copy.248 = f32[5,512,512]{2,1,0:T(8,128)} copy(f32[5,512,512]{2,1,0:T(8,128)} %all-reduce.2.cloned.1.call-done) | data formatting | bytes 10485760
  (277 shorter events, 71.6 us)
Async XLA Ops:
  7.2 259.2 %copy-start = (bf16[512,512]{1,0:T(8,128)(2,1)S(1)}, bf16[512,512]{1,0:T(8,128)(2,1)}, u32[]{:S(2)}) copy-start(bf16[512,512]{1,0:T(8,128)(2,1)} %param.22) | copy-start | bytes 1572868
  7.2 34.3 %all-gather.6.cloned.1.call-start = ((), (), s32[]{:S(2)}) async-start(), calls=%async_computation.5 | async-start | bytes 2359296 | tf_op jit(solution)/shard_map/all_gather | solution.py:154
  10.8 1.5 copy-start.1
  11.0 1.3 copy-start.19
  11.1 2.3 copy-start.21
  11.4 2.1 copy-start.6
  12.3 56.8 %all-gather.4.cloned.1.call-start = ((), (), s32[]{:S(2)}) async-start(), calls=%async_computation.4 | async-start | bytes 2359296 | tf_op jit(solution)/shard_map/all_gather | solution.py:155
  13.4 267.7 %reduce-scatter.3.cloned.1.call-start = ((), (), s32[]{:S(2)}) async-start(), calls=%async_computation.6 | async-start | bytes 2359296 | tf_op jit(solution)/shard_map/reduce_scatter | solution.py:192
  14.0 3.1 copy-start.3
  14.0 4.3 copy-start.44
  14.0 17.5 %copy-start.49 = (s32[1,8]{1,0:T(1,128)S(1)}, s32[1,8]{1,0:T(1,128)}, u32[]{:S(2)}) copy-start(s32[1,8]{1,0:T(1,128)} %param.24) | copy-start | bytes 100
  14.1 19.2 %copy-start.7 = (bf16[256,512]{1,0:T(8,128)(2,1)S(1)}, bf16[256,512]{1,0:T(8,128)(2,1)}, u32[]{:S(2)}) copy-start(bf16[256,512]{1,0:T(8,128)(2,1)} %param.29) | copy-start | bytes 786436
  14.1 19.2 %copy-start.17 = (bf16[512,512]{1,0:T(8,128)(2,1)S(1)}, bf16[512,512]{1,0:T(8,128)(2,1)}, u32[]{:S(2)}) copy-start(bf16[512,512]{1,0:T(8,128)(2,1)} %param.21) | copy-start | bytes 1572868
  90.5 1.8 copy-start.24
  90.5 2.1 copy-start.37
  90.5 2.1 copy-start.43
  92.6 1.0 copy-start.36
  92.6 0.9 copy-start.42
  93.4 1.0 copy-start.35
  93.4 1.0 copy-start.41
  94.3 1.0 copy-start.34
  94.3 1.0 copy-start.40
  95.1 1.0 copy-start.33
  95.2 1.0 copy-start.39
  96.0 1.0 copy-start.32
  96.1 1.0 copy-start.38
  96.9 1.0 copy-start.31
  99.5 1.0 copy-start.23
  99.8 1.0 copy-start.30
  195.4 0.7 copy-start.45
  196.1 7.5 %copy-start.50 = (s32[16]{0:T(128)S(1)}, s32[16]{0:T(128)}, u32[]{:S(2)}) copy-start(s32[16]{0:T(128)} %param.26) | copy-start | bytes 196
  205.2 63.5 %all-to-all-start = ((bf16[16,128,512]{2,1,0:T(8,128)(2,1)}), bf16[16,128,512]{2,1,0:T(8,128)(2,1)}, u32[]{:S(2)}, u32[]{:S(2)}) async-start(bf16[16,128,512]{2,1,0:T(8,128)(2,1)} %broadcast_select_fusion), calls=%async_computation | async-start | bytes 4194304 | tf_op jit(solution)/shard_map/all_to_all | solution.py:131
  211.8 0.7 copy-start.47
  211.8 0.7 copy-start.48
  211.8 80.8 %reduce-scatter.5.cloned.1.call-start = ((), (), s32[]{:S(2)}) async-start(), calls=%async_computation.7 | async-start | bytes 2359296 | tf_op jit(solution)/shard_map/reduce_scatter | solution.py:198
  236.1 30.3 %copy-start.8 = (bf16[256,512]{1,0:T(8,128)(2,1)S(1)}, bf16[256,512]{1,0:T(8,128)(2,1)}, u32[]{:S(2)}) copy-start(bf16[256,512]{1,0:T(8,128)(2,1)} %param.29) | copy-start | bytes 786436
  237.5 31.2 %copy-start.25 = (bf16[2048,256]{1,0:T(8,128)(2,1)}, bf16[2048,256]{1,0:T(8,128)(2,1)S(1)}, u32[]{:S(2)}) copy-start(bf16[2048,256]{1,0:T(8,128)(2,1)S(1)} %convert_element_type.131) | copy-start | bytes 3145732
  268.8 33.4 %all-to-all-start.1 = ((bf16[16,128,512]{2,1,0:T(8,128)(2,1)}), bf16[16,128,512]{2,1,0:T(8,128)(2,1)S(1)}, u32[]{:S(2)}, u32[]{:S(2)}) async-start(bf16[16,128,512]{2,1,0:T(8,128)(2,1)} %bitcast.233), calls=%async_computation.3 | async-start | bytes 4194304 | tf_op jit(solution)/shard_map/all_to_all | solution.py:216
  275.4 179.9 %all-reduce.2.cloned.1.call-start = ((), (), s32[]{:S(2)}) async-start(), calls=%async_computation.8 | async-start | bytes 10485760 | tf_op jit(solution)/shard_map/psum | solution.py:242
  275.4 3.4 copy-start.4
  279.0 0.7 copy-start.11
  281.1 8.1 %copy-start.2 = (f32[256,512]{1,0:T(8,128)S(1)}, f32[256,512]{1,0:T(8,128)}, u32[]{:S(2)}) copy-start(f32[256,512]{1,0:T(8,128)} %copy-done.1) | copy-start | bytes 1572868
  290.6 0.7 copy-start.13
  291.4 3.6 copy-start.9
  291.4 3.6 copy-start.27
  292.7 3.6 copy-start.28
  297.5 0.9 copy-start.5
  297.5 1.0 copy-start.29
  299.7 5.1 %copy-start.12 = (bf16[256,8,64]{0,2,1:T(8,128)(2,1)S(1)}, bf16[256,8,64]{0,2,1:T(8,128)(2,1)}, u32[]{:S(2)}) copy-start(bf16[256,8,64]{0,2,1:T(8,128)(2,1)} %copy-done.11) | copy-start | bytes 786436
  302.2 2.5 copy-start.22
  302.2 2.9 copy-start.16
  302.2 2.9 copy-start.18
  304.7 1.4 copy-start.14
  304.7 1.4 copy-start.15
  304.7 1.8 copy-start.20
  304.7 1.8 copy-start.26
  306.9 13.6 %copy-start.46 = (f32[512]{0:T(512)S(1)}, f32[512]{0:T(512)}, u32[]{:S(2)}) copy-start(f32[512]{0:T(512)} %param.17) | copy-start | bytes 6148
  306.9 79.6 %copy-start.10 = (bf16[256,512]{1,0:T(8,128)(2,1)S(1)}, bf16[256,512]{1,0:T(8,128)(2,1)}, u32[]{:S(2)}) copy-start(bf16[256,512]{1,0:T(8,128)(2,1)} %param.29) | copy-start | bytes 786436
Sparse Core Ops, SparseCore 0:
  12.4 29.0 all-gather.5
  43.2 25.8 all-gather.3
  195.5 30.9 reduce-scatter.2
  228.8 32.8 reduce-scatter.4
  297.7 157.5 all-reduce.1
where the time goes:
time: 470 us; the launch traced here: 468 us
  waiting for transfers between devices  102 us (22%)
  local copies, waits for them, and re-layouts  97.6 us (21%)
  other arithmetic  84.2 us (18%)
  blocking collectives  78.9 us (17%)
  matrix products  70.8 us (15%)
  between operations  14.7 us (3%)
  starting transfers between devices  13.4 us (3%)
  loops' own time  5.81 us (1%)
    psum x1, waiting for transfers between devices, local(): weight_sums, gain_sum = lax.psum((weight_terms, gain_term), ('dom', 'blk'))  67.9 us
    psum x1, blocking collectives, local(): weight_sums, gain_sum = lax.psum((weight_terms, gain_term), ('dom', 'blk'))  65.8 us
    scatter-add x1, other arithmetic, local(): jax.ops.segment_sum(jnp.ones(edge_dst.shape, jnp.float32), edge_dst, row_...  28.8 us
    all_gather x1, waiting for transfers between devices, local(): lax.all_gather(value_flat, 'blk', axis=0, tiled=True)  23.3 us
    scatter-add x1, other arithmetic, local(): jnp.zeros((peer_count * slot_count * row_count,), jnp.int32).at[pair_index]  22.4 us
    unnamed x106, local copies, waits for them, and re-layouts  20.3 us
    dot_general x16, matrix products, block_weights(): jnp.einsum('rhe,khe->hrk', query_heads, key_heads, preferred_element_type...  19.7 us
    slice x9, local copies, waits for them, and re-layouts, attend_piece(): value_rows[first_row:last_row].reshape(part_rows, HEADS, HEAD_DIM)  13.6 us
  transfers between devices with their start and end apart: 7, of which 4 were waited for; matrix products, arithmetic and copies ran while one was open for 25% of the time, Pallas kernels for 0%

commit v1 on v0

--- a/solution.py
+++ b/solution.py
@@ -8,6 +8,11 @@
 HEAD_DIM = 64
 epsilon = 1e-06
 score_shift = 8.0
+
+
+def swapped_in(block, mesh_axis, d):
+    sent = jnp.stack([block] * lax.axis_size(mesh_axis))
+    return jnp.concatenate(lax.all_to_all(sent, mesh_axis, 0, 0), axis=d)
 
 
 def settle(array):
@@ -152,7 +157,7 @@
     key_set = None
     key_set = (
         lax.all_gather(key_flat, "blk", axis=0, tiled=True),
-        lax.all_gather(value_flat, "blk", axis=0, tiled=True),
+        swapped_in(value_flat, "blk", 0),
         lax.all_gather(node_cluster, "blk", axis=0, tiled=True),
     )
     numer, denom = fold_step(start_state, key_set, 0)

time: 470 us -> 445 us (0.947)
  waiting for transfers between devices: 102 us -> 69.9 us
  local copies, waits for them, and re-layouts: 97.6 us -> 79.9 us
  blocking collectives: 78.9 us -> 92.2 us
  starting transfers between devices: 13.4 us -> 20.3 us
    all_gather x1 -> x0, waiting for transfers between devices: 23.3 us -> none  [local(): lax.all_gather(value_flat, 'blk', axis=0, tiled=True)]
    all_gather x1, blocking collectives: 13.1 us -> 26.4 us  [local(): lax.all_gather(node_cluster, 'blk', axis=0, tiled=True)]
    slice x9 -> x1, local copies, waits for them, and re-layouts: 13.6 us -> 1.36 us  [attend_piece(): value_rows[first_row:last_row].reshape(part_rows, HEADS, HEAD_DIM)]
    all_gather x1, waiting for transfers between devices: 7.86 us -> 0.01 us  [local(): lax.all_gather(key_flat, 'blk', axis=0, tiled=True)]
    all_to_all x0 -> x1, starting transfers between devices: none -> 6.81 us  [swapped_in(): return jnp.concatenate(lax.all_to_all(sent, mesh_axis, 0, 0), axis=d)]
    reshape x1 -> x0, local copies, waits for them, and re-layouts: 6.14 us -> none  [local(): value_rows.reshape(block_count, row_count, HEADS, HEAD_DIM)]
    unnamed x106 -> x119, local copies, waits for them, and re-layouts: 20.3 us -> 16.1 us
  transfers between devices with their start and end apart: 7 -> 7, of which waited for: 4 -> 2; matrix products, arithmetic and copies ran while one was open for 25% -> 28% of each run, Pallas kernels for 0% -> 0%
where the time goes in v1:
time: 445 us; the launch traced here: 443 us
  blocking collectives  92.2 us (21%)
  other arithmetic  86.1 us (19%)
  local copies, waits for them, and re-layouts  79.9 us (18%)
  matrix products  73.9 us (17%)
  waiting for transfers between devices  69.9 us (16%)
  starting transfers between devices  20.3 us (5%)
  between operations  14.7 us (3%)
  loops' own time  5.81 us (1%)
    psum x1, waiting for transfers between devices, local(): weight_sums, gain_sum = lax.psum((weight_terms, gain_term), ('dom', 'blk'))  66.1 us
    psum x1, blocking collectives, local(): weight_sums, gain_sum = lax.psum((weight_terms, gain_term), ('dom', 'blk'))  65.8 us
    scatter-add x1, other arithmetic, local(): jax.ops.segment_sum(jnp.ones(edge_dst.shape, jnp.float32), edge_dst, row_...  28.8 us
    all_gather x1, blocking collectives, local(): lax.all_gather(node_cluster, 'blk', axis=0, tiled=True)  26.4 us
    scatter-add x1, other arithmetic, local(): jnp.zeros((peer_count * slot_count * row_count,), jnp.int32).at[pair_index]  22.4 us
    dot_general x16, matrix products, block_weights(): jnp.einsum('rhe,khe->hrk', query_heads, key_heads, preferred_element_type...  19.7 us
    unnamed x119, local copies, waits for them, and re-layouts  16.1 us
    scatter-add x1, other arithmetic, local(): jax.ops.segment_sum(returned.reshape(peer_count * slot_count, feat_width)...  13.7 us
  transfers between devices with their start and end apart: 7, of which 2 were waited for; matrix products, arithmetic and copies ran while one was open for 28% of the time, Pallas kernels for 0%

profile of v1, /device:TPU:1, one launch (start us, length us, event | category | flops | bytes accessed | tf_op | source)
XLA Modules:
  0.0 442.7 jit_solution(4552694515817896444)
XLA Ops:
  9.5 1.3 fusion.57
  12.7 1.5 stack.14
  14.2 6.8 %all-to-all-start.1 = ((bf16[8,256,512]{1,2,0:T(8,128)(2,1)}), bf16[8,256,512]{1,2,0:T(8,128)(2,1)S(1)}, u32[]{:S(2)}, u32[]{:S(2)}) async-start(bf16[8,256,512]{1,2,0:T(8,128)(2,1)} %stack.14), calls=%async_computation.1 | async-start | bytes 4194304 | tf_op jit(solution)/shard_map/all_to_all | solution.py:15
  21.0 2.2 fusion.66
  23.1 2.0 copy.125
  27.1 2.0 copy.126
  29.2 2.0 multiply_convert_fusion.1
  31.2 1.8 copy.127
  33.0 26.4 %all-gather = s32[8,1,256]{2,1,0:T(1,128)S(1)} all-gather(s32[1,1,256]{2,1,0:T(1,128)S(1)} %bitcast.260), channel_id=1, replica_groups=mesh['dom'=16,'blk'=8] {'blk'}, dimensions={0}, use_global_device_ids=true | all-gather | bytes 9216 | tf_op jit(solution)/shard_map/all_gather | solution.py:161
  59.6 1.5 compare_and_fusion.1
  61.2 2.3 fusion.67
  63.5 1.4 fusion.55
  64.8 2.9 fusion.54
  67.8 1.9 copy.130
  69.7 1.8 copy.132
  71.5 1.8 copy.134
  73.3 1.8 copy.136
  77.1 1.7 fusion.64
  89.5 6.1 %reshape.809 = bf16[8,256,8,64]{3,2,1,0:T(8,128)(2,1)} reshape(bf16[2048,512]{1,0:T(8,128)(2,1)} %all-gather.3.cloned.1.call-done) | data formatting | bytes 4194304 | tf_op jit(solution)/shard_map/reshape | solution.py:187
  95.6 5.1 %copy.148 = bf16[8,256,8,64]{1,3,2,0:T(8,128)(2,1)} copy(bf16[8,256,8,64]{3,2,1,0:T(8,128)(2,1)} %reshape.809) | data formatting | bytes 4194304
  100.7 66.8 %while.17 = (s32[]{:T(128)}, f32[256,8,64]{0,2,1:T(8,128)S(1)}, bf16[8,256,512]{1,2,0:T(8,128)(2,1)}, bf16[8,256,512]{2,1,0:T(8,128)(2,1)}, bf16[8,256,8,64]{1,3...) while((s32[]{:T(128)}, f32[256,8,64]{0,2,1:T(8,128)S(1)}, ...), condition=%wide.region_23.24_spmd.clone, body=%wide.region_22.23_spmd.clone.sunk | while | flops 340262912 | bytes 15088305 | solution.py:193
  102.1 1.6 bitcast_select_fusion.2
  103.7 1.4 fusion.163
  107.7 1.2 fusion.164
  110.5 1.6 bitcast_select_fusion.2
  112.1 1.4 fusion.163
  118.8 1.6 bitcast_select_fusion.2
  120.4 1.4 fusion.163
  127.2 1.6 bitcast_select_fusion.2
  128.8 1.4 fusion.163
  135.5 1.6 bitcast_select_fusion.2
  137.1 1.4 fusion.163
  143.9 1.6 bitcast_select_fusion.2
  145.5 1.4 fusion.163
  149.4 1.2 fusion.164
  152.3 1.6 bitcast_select_fusion.2
  153.9 1.4 fusion.163
  160.6 1.6 bitcast_select_fusion.2
  162.2 1.4 fusion.163
  167.6 4.0 copy.149
  172.3 7.5 %gather_fusion = bf16[2048,512]{1,0:T(8,128)(2,1)S(1)} fusion(bf16[256,512]{1,0:T(8,128)(2,1)S(1)} %fusion.38, s32[2048]{0:T(1024)S(1)} %fusion.48), kind=kCustom, calls=%fused_computation | custom fusion | bytes 4202496 | tf_op jit(solution)/shard_map/gather | solution.py:135
  179.9 1.5 broadcast_select_fusion
  181.4 6.8 %all-to-all-start = ((bf16[16,128,512]{2,1,0:T(8,128)(2,1)}), bf16[16,128,512]{2,1,0:T(8,128)(2,1)}, u32[]{:S(2)}, u32[]{:S(2)}) async-start(bf16[16,128,512]{2,1,0:T(8,128)(2,1)} %broadcast_select_fusion), calls=%async_computation | async-start | bytes 4194304 | tf_op jit(solution)/shard_map/all_to_all | solution.py:136
  189.0 22.4 %scatter_custom_fusion = s32[524288]{0:T(1024)S(1)} fusion(s32[4096]{0:T(1024)S(1)} %compare_select_fusion, s32[4096]{0:T(1024)S(1)} %broadcast.738, s32[]{:T(128)} %constant.148.clone.1), kind=kCustom, calls=%fused_computation.77 | custom fusion | flops 4096 | bytes 2097156 | tf_op jit(solution)/shard_map/scatter-add | solution.py:166
  212.6 1.5 convert_element_type.131
  214.0 28.8 %scatter_custom_fusion.1 = f32[256]{0:T(256)S(1)} fusion(s32[4096]{0:T(1024)S(1)} %copy-done.55, f32[4096]{0:T(1024)S(1)} %broadcast.739, f32[]{:T(128)} %constant.152.clone.1), kind=kCustom, calls=%fused_computation.188 | custom fusion | flops 4096 | bytes 1028 | tf_op jit(solution)/shard_map/scatter-add | solution.py:169
  242.8 2.4 convolution_convert_fusion
  245.2 6.6 %all-to-all-start.2 = ((bf16[16,128,512]{2,1,0:T(8,128)(2,1)}), bf16[16,128,512]{2,1,0:T(8,128)(2,1)S(1)}, u32[]{:S(2)}, u32[]{:S(2)}) async-start(bf16[16,128,512]{2,1,0:T(8,128)(2,1)} %bitcast.235), calls=%async_computation.4 | async-start | bytes 4194304 | tf_op jit(solution)/shard_map/all_to_all | solution.py:221
  251.9 3.4 fusion.21
  256.2 1.3 fusion.18
  257.5 2.1 convert_multiply_fusion.4
  259.6 2.1 copy.151
  263.6 2.1 copy.152
  265.7 1.5 fusion.41
  267.9 1.3 fusion.17
  269.2 2.3 fusion.16
  271.5 1.3 fusion.15
  272.7 1.3 fusion.14
  276.1 3.0 all-to-all-done.2
  279.2 2.3 convert_select_fusion
  283.7 13.7 %scatter_fusion = f32[256,512]{1,0:T(8,128)S(1)} fusion(f32[256,512]{1,0:T(8,128)S(1)} %convolution_add_fusion.7, s32[2048]{0:T(1024)S(1)} %bitcast.261, f32[2048,512]{1,0:T(8,128)} %bitcast.219), kind=kCustom, calls=%fused_computation.3 | custom fusion | flops 1048576 | bytes 12591104 | tf_op jit(solution)/shard_map/scatter-add | solution.py:229
  297.6 65.8 %psum.15 = f32[512]{0:T(512)} all-reduce(f32[512]{0:T(512)S(1)} %get-tuple-element.245), channel_id=1, replica_groups=mesh['dom'=16,'blk'=8] {'dom','blk'}, use_global_device_ids=true, to_apply=%region_32.33 | all-reduce | flops 512 | bytes 4096 | tf_op jit(solution)/shard_map/psum | solution.py:247
  364.3 66.1 %all-reduce.2.cloned.1.call-done = f32[5,512,512]{2,1,0:T(8,128)} async-done(((f32[5,512,512]{2,1,0:T(8,128)}), f32[5,512,512]{2,1,0:T(8,128)}) %all-reduce.2.cloned.1.call-update) | async-done | bytes 5242896 | tf_op jit(solution)/shard_map/psum | solution.py:247
  430.4 5.8 %copy.211 = f32[5,512,512]{2,1,0:T(8,128)} copy(f32[5,512,512]{2,1,0:T(8,128)} %all-reduce.2.cloned.1.call-done) | data formatting | bytes 10485760
  (282 shorter events, 64.3 us)
Async XLA Ops:
  7.2 235.7 %copy-start = (bf16[512,512]{1,0:T(8,128)(2,1)S(1)}, bf16[512,512]{1,0:T(8,128)(2,1)}, u32[]{:S(2)}) copy-start(bf16[512,512]{1,0:T(8,128)(2,1)} %param.22) | copy-start | bytes 1572868
  7.2 57.7 %all-gather.3.cloned.1.call-start = ((), (), s32[]{:S(2)}) async-start(), calls=%async_computation.5 | async-start | bytes 2359296 | tf_op jit(solution)/shard_map/all_gather | solution.py:159
  10.8 1.4 copy-start.3
  11.0 1.2 copy-start.18
  11.3 2.8 copy-start.7
  14.2 49.3 %all-to-all-start.1 = ((bf16[8,256,512]{1,2,0:T(8,128)(2,1)}), bf16[8,256,512]{1,2,0:T(8,128)(2,1)S(1)}, u32[]{:S(2)}, u32[]{:S(2)}) async-start(bf16[8,256,512]{1,2,0:T(8,128)(2,1)} %stack.14), calls=%async_computation.1 | async-start | bytes 4194304 | tf_op jit(solution)/shard_map/all_to_all | solution.py:15
  21.0 236.6 %reduce-scatter.3.cloned.1.call-start = ((), (), s32[]{:S(2)}) async-start(), calls=%async_computation.6 | async-start | bytes 2359296 | tf_op jit(solution)/shard_map/reduce_scatter | solution.py:197
  25.2 7.8 %copy-start.51 = (s32[256]{0:T(256)S(1)}, s32[256]{0:T(256)}, u32[]{:S(2)}) copy-start(s32[256]{0:T(256)} %param.23) | copy-start | bytes 3076
  25.2 34.3 %copy-start.56 = (s32[1,8]{1,0:T(1,128)S(1)}, s32[1,8]{1,0:T(1,128)}, u32[]{:S(2)}) copy-start(s32[1,8]{1,0:T(1,128)} %param.24) | copy-start | bytes 100
  63.5 4.3 copy-start.1
  67.7 7.4 %copy-start.32 = (bf16[256,512]{1,0:T(8,128)(2,1)S(1)}, bf16[256,512]{1,0:T(8,128)(2,1)}, u32[]{:S(2)}) copy-start(bf16[256,512]{1,0:T(8,128)(2,1)} %get-tuple-element.282) | copy-start | bytes 786436
  67.7 8.2 %copy-start.31 = (bf16[256,512]{1,0:T(8,128)(2,1)S(1)}, bf16[256,512]{1,0:T(8,128)(2,1)}, u32[]{:S(2)}) copy-start(bf16[256,512]{1,0:T(8,128)(2,1)} %get-tuple-element.281) | copy-start | bytes 786436
  67.7 9.1 %copy-start.30 = (bf16[256,512]{1,0:T(8,128)(2,1)S(1)}, bf16[256,512]{1,0:T(8,128)(2,1)}, u32[]{:S(2)}) copy-start(bf16[256,512]{1,0:T(8,128)(2,1)} %get-tuple-element.280) | copy-start | bytes 786436
  67.8 9.2 %copy-start.29 = (bf16[256,512]{1,0:T(8,128)(2,1)S(1)}, bf16[256,512]{1,0:T(8,128)(2,1)}, u32[]{:S(2)}) copy-start(bf16[256,512]{1,0:T(8,128)(2,1)} %get-tuple-element.279) | copy-start | bytes 786436
  67.8 9.3 %copy-start.2 = (bf16[256,512]{0,1:T(8,128)(2,1)S(1)}, bf16[256,512]{0,1:T(8,128)(2,1)}, u32[]{:S(2)}) copy-start(bf16[256,512]{0,1:T(8,128)(2,1)} %copy.127) | copy-start | bytes 786436
  76.9 1.9 copy-start.28
  77.1 2.1 copy-start.44
  77.1 2.1 copy-start.50
  79.2 1.0 copy-start.43
  79.2 0.9 copy-start.49
  80.0 1.0 copy-start.42
  80.0 1.0 copy-start.48
  80.9 1.0 copy-start.41
  80.9 1.0 copy-start.47
  81.7 1.0 copy-start.40
  81.7 1.0 copy-start.46
  82.6 0.9 copy-start.45
  84.3 1.0 copy-start.27
  85.0 1.0 copy-start.26
  85.2 1.1 copy-start.25
  86.0 1.0 copy-start.24
  86.3 1.0 copy-start.23
  87.0 1.0 copy-start.22
  87.3 1.1 copy-start.21
  87.3 1.1 copy-start.39
  172.3 7.5 %copy-start.57 = (s32[16]{0:T(128)S(1)}, s32[16]{0:T(128)}, u32[]{:S(2)}) copy-start(s32[16]{0:T(128)} %param.26) | copy-start | bytes 196
  181.4 63.8 %all-to-all-start = ((bf16[16,128,512]{2,1,0:T(8,128)(2,1)}), bf16[16,128,512]{2,1,0:T(8,128)(2,1)}, u32[]{:S(2)}, u32[]{:S(2)}) async-start(bf16[16,128,512]{2,1,0:T(8,128)(2,1)} %broadcast_select_fusion), calls=%async_computation | async-start | bytes 4194304 | tf_op jit(solution)/shard_map/all_to_all | solution.py:136
  188.2 0.8 copy-start.54
  188.2 0.8 copy-start.55
  188.3 80.9 %reduce-scatter.5.cloned.1.call-start = ((), (), s32[]{:S(2)}) async-start(), calls=%async_computation.7 | async-start | bytes 2359296 | tf_op jit(solution)/shard_map/reduce_scatter | solution.py:203
  212.6 30.3 %copy-start.8 = (bf16[256,512]{1,0:T(8,128)(2,1)S(1)}, bf16[256,512]{1,0:T(8,128)(2,1)}, u32[]{:S(2)}) copy-start(bf16[256,512]{1,0:T(8,128)(2,1)} %param.29) | copy-start | bytes 786436
  214.0 31.2 %copy-start.33 = (bf16[2048,256]{1,0:T(8,128)(2,1)}, bf16[2048,256]{1,0:T(8,128)(2,1)S(1)}, u32[]{:S(2)}) copy-start(bf16[2048,256]{1,0:T(8,128)(2,1)S(1)} %convert_element_type.131) | copy-start | bytes 3145732
  245.2 34.0 %all-to-all-start.2 = ((bf16[16,128,512]{2,1,0:T(8,128)(2,1)}), bf16[16,128,512]{2,1,0:T(8,128)(2,1)S(1)}, u32[]{:S(2)}, u32[]{:S(2)}) async-start(bf16[16,128,512]{2,1,0:T(8,128)(2,1)} %bitcast.235), calls=%async_computation.4 | async-start | bytes 4194304 | tf_op jit(solution)/shard_map/all_to_all | solution.py:221
  251.9 178.5 %all-reduce.2.cloned.1.call-start = ((), (), s32[]{:S(2)}) async-start(), calls=%async_computation.8 | async-start | bytes 10485760 | tf_op jit(solution)/shard_map/psum | solution.py:247
  251.9 3.4 copy-start.5
  255.5 0.7 copy-start.11
  257.5 8.1 %copy-start.4 = (f32[256,512]{1,0:T(8,128)S(1)}, f32[256,512]{1,0:T(8,128)}, u32[]{:S(2)}) copy-start(f32[256,512]{1,0:T(8,128)} %copy-done.3) | copy-start | bytes 1572868
  267.2 0.7 copy-start.13
  267.9 3.6 copy-start.9
  267.9 3.6 copy-start.35
  269.2 3.6 copy-start.37
  274.0 0.9 copy-start.6
  274.0 1.0 copy-start.38
  276.1 5.4 %copy-start.12 = (bf16[256,8,64]{0,2,1:T(8,128)(2,1)S(1)}, bf16[256,8,64]{0,2,1:T(8,128)(2,1)}, u32[]{:S(2)}) copy-start(bf16[256,8,64]{0,2,1:T(8,128)(2,1)} %copy-done.11) | copy-start | bytes 786436
  279.2 2.3 copy-start.20
  279.2 2.7 copy-start.16
  279.2 2.7 copy-start.17
  279.2 2.7 copy-start.36
  281.5 1.5 copy-start.14
  281.5 1.5 copy-start.15
  281.5 1.8 copy-start.19
  281.5 1.8 copy-start.34
  283.7 13.7 %copy-start.53 = (f32[512]{0:T(512)S(1)}, f32[512]{0:T(512)}, u32[]{:S(2)}) copy-start(f32[512]{0:T(512)} %param.17) | copy-start | bytes 6148
  283.7 79.7 %copy-start.10 = (bf16[256,512]{1,0:T(8,128)(2,1)S(1)}, bf16[256,512]{1,0:T(8,128)(2,1)}, u32[]{:S(2)}) copy-start(bf16[256,512]{1,0:T(8,128)(2,1)} %param.29) | copy-start | bytes 786436
  (1 other events, 0.7 us)
Sparse Core Ops, SparseCore 0:
  12.4 37.7 all-gather.2
  171.7 30.0 reduce-scatter.2
  204.2 32.7 reduce-scatter.4
  274.2 156.1 all-reduce.1
